TPU v7x, 256 devices: a whole 4x4x8 slice. The times are simulated.
256 devices in a mesh: lev: 8 (over z_lo, x), hor: 32 (over z_hi, y, core).
Axes of the slice: x: 4, y: 4, z: 8 (z_hi: 4, z_lo: 2; z = z_hi * 2 + z_lo), core: 2. Of those that a mesh axis runs over, the one named last changes fastest.
Arguments:
- slab_fields: float32 [4, 32, 524288], P(None, 'lev', 'hor'), may hold values from -6 to 6
- sample_index: int32 [32, 1024], P('hor', 'lev'), may hold values from 0 to 2047
- thickness: float32 [32], replicated, may hold values from 0.3 to 3
- level_cuts: int32 [31], replicated, may hold values 0 or 1
Outputs:
- gram: float32 [2176, 2176], P('hor', 'lev')
Inputs may be any that keep to these rules, and one draw needn't show every extreme that they name: sample_index[j, k] indexes a column among the 2048 columns that start at j * 16384 + (k // 128) * 2048.
All inputs are finite; a program needn't handle non-finite values.
Results may differ from a plain program's by a relative error of at most 0.00068.
Values may be sent and summed in bfloat16 or wider, within the bound.
No kernel may reach another device: no remote copies, remote signals or barrier semaphores. Data moves between devices by JAX's collectives and lax.ppermute only.
A program may use at most 128 MiB of HBM per device.

v0:
```python
import jax
import jax.numpy as jnp
from jax import lax
from jax.sharding import PartitionSpec as P


def vertical_filter(values, thickness, level_cuts):
    link = 1.0 - level_cuts.astype(jnp.float32)
    zero_one = jnp.zeros((1,), jnp.float32)
    lower_link = jnp.concatenate([zero_one, link])
    upper_link = jnp.concatenate([link, zero_one])
    lower_weight = jnp.concatenate([zero_one, thickness[:-1]]) * lower_link
    upper_weight = jnp.concatenate([thickness[1:], zero_one]) * upper_link
    zero_row = jnp.zeros_like(values[:, :1, :])
    below = jnp.concatenate([zero_row, values[:, :-1, :]], axis=1)
    above = jnp.concatenate([values[:, 1:, :], zero_row], axis=1)
    numer = (
        2.0 * thickness[None, :, None] * values
        + lower_weight[None, :, None] * below
        + upper_weight[None, :, None] * above
    )
    denom = 2.0 * thickness + lower_weight + upper_weight
    return numer / denom[None, :, None]


def quadratic_features(smooth):
    count = smooth.shape[2]
    later = jnp.concatenate([smooth[2], smooth[3]], axis=0)
    earlier = jnp.concatenate([smooth[0], smooth[1]], axis=0)
    product = (later[:, None, :] * smooth[0][None, :, :]).reshape(-1, count)
    return jnp.concatenate([later, earlier, product], axis=0).astype(jnp.bfloat16)


def on_device(slab_fields, sample_index, thickness, level_cuts):
    samp_count = sample_index.shape[1]
    lev_count = lax.axis_size("lev")
    hor_count = lax.axis_size("hor")
    all_lists = lax.all_gather(sample_index, "lev", axis=1, tiled=True)[0]
    group_cols = slab_fields.shape[2] // lev_count
    offsets = jnp.arange(all_lists.shape[0]) // samp_count * group_cols + all_lists
    chosen = jnp.take(slab_fields, offsets, axis=2)
    picked_cols = lax.all_to_all(chosen, "lev", split_axis=2, concat_axis=1, tiled=True)
    smooth = vertical_filter(picked_cols, thickness, level_cuts)
    feat_count = 4 * smooth.shape[1] + 2 * smooth.shape[1] * smooth.shape[1]
    col_count = feat_count // lev_count
    col_start = lax.axis_index("lev") * col_count
    features_bf = quadratic_features(smooth)
    block_features_bf = lax.all_gather(features_bf, "lev", axis=1, tiled=True)
    chosen_rows = lax.dynamic_slice_in_dim(block_features_bf, col_start, col_count, 0)
    column_block = lax.dot_general(
        block_features_bf, chosen_rows, (((1,), (1,)), ((), ())), preferred_element_type=jnp.float32
    )
    gram_block = lax.psum_scatter(column_block, "hor", scatter_dimension=0, tiled=True)
    count_all = samp_count * lev_count * hor_count
    return gram_block / count_all


def solution(mesh):
    in_specs = (P(None, "lev", "hor"), P("hor", "lev"), P(), P())
    out_specs = P("hor", "lev")
    return jax.shard_map(
        on_device, mesh=mesh, in_specs=in_specs, out_specs=out_specs, check_vma=False
    )
```

profile of v0, /device:TPU:26, one launch (start us, length us, event | category | flops | bytes accessed | tf_op | source)
XLA Modules:
  0.0 281.2 jit_solution(17869697223792710759)
XLA Ops:
  6.5 21.7 %copy.7 = f32[4,4,16384]{1,0,2:T(4,128)} copy(f32[4,4,16384]{2,1,0:T(4,128)} %param.4) | data formatting | bytes 2097152 | tf_op args[0]
  28.3 16.4 %all_gather.6 = s32[1,1024]{1,0:T(1,128)S(1)} all-gather(s32[1,128]{1,0:T(1,128)S(1)} %copy-done.2), channel_id=1, replica_groups=mesh['lev'=8,'hor'=32] {'lev'}, dimensions={1}, use_global_device_ids=true | all-gather | bytes 4608 | tf_op jit(solution)/shard_map/all_gather | solution.py:38
  44.7 16.8 %gather_fusion = f32[1024,4,4]{2,1,0:T(4,128)} fusion(f32[4,4,16384]{1,0,2:T(4,128)} %copy.7, s32[1024]{0:T(1024)S(1)} %broadcast_clamp_fusion), kind=kCustom, calls=%fused_computation | custom fusion | bytes 135168 | tf_op jit(solution)/shard_map/jit(_take)/gather | solution.py:41
  61.5 5.5 %fusion.18 = f32[1024,4,4]{2,1,0:T(4,128)S(1)} fusion(f32[1024,4,4]{2,1,0:T(4,128)} %gather_fusion, pred[1024]{0:T(1024)(128)(4,1)S(1)} %compare_and_fusion), kind=kLoop, calls=%fused_computation.49 | loop fusion | flops 16384 | bytes 132096
  67.0 3.0 %reshape.135 = f32[8,1,2048]{2,1,0:T(1,128)} reshape(f32[1024,4,4]{2,1,0:T(4,128)S(1)} %fusion.18) | data formatting | bytes 131072
  70.1 6.6 %all-to-all-start = ((f32[8,1,2048]{2,1,0:T(1,128)}), f32[8,1,2048]{2,1,0:T(1,128)S(1)}, u32[]{:S(2)}, u32[]{:S(2)}) async-start(f32[8,1,2048]{2,1,0:T(1,128)} %reshape.135), calls=%async_computation | async-start | bytes 131072 | tf_op jit(solution)/shard_map/all_to_all | solution.py:42
  76.7 0.1 fusion.17
  76.7 0.1 add_add_fusion
  76.8 4.8 %all-to-all-done = f32[8,1,2048]{2,1,0:T(1,128)S(1)} async-done(((f32[8,1,2048]{2,1,0:T(1,128)}), f32[8,1,2048]{2,1,0:T(1,128)S(1)}, u32[]{:S(2)}, u32[]{:S(2)}) %all-to-all-start) | async-done | bytes 65568 | tf_op jit(solution)/shard_map/all_to_all | solution.py:42
  81.6 0.5 broadcast.122
  82.1 0.8 reduce
  82.9 2.7 reshape.136
  85.6 0.8 copy.8
  86.5 0.1 add_divide_fusion
  86.6 0.1 multiply_convert_fusion
  86.7 0.1 constant_dynamic-update-slice_fusion
  86.8 0.8 copy-done
  87.6 0.0 all-gather.2.cloned.1.call-update
  87.7 64.6 %all-gather.2.cloned.1.call-done = bf16[2176,1024]{1,0:T(8,128)(2,1)} async-done(((bf16[2176,128]{1,0:T(8,128)(2,1)}), bf16[2176,1024]{1,0:T(8,128)(2,1)}) %all-gather.2.cloned.1.call-update) | async-done | bytes 4456464 | tf_op jit(solution)/shard_map/all_gather | solution.py:48
  152.2 4.9 %fusion.1 = f32[2176,272]{1,0:T(8,128)S(1)} fusion(bf16[2176,1024]{1,0:T(8,128)(2,1)} %all-gather.2.cloned.1.call-done, s32[]{:T(128)S(6)} %select_n.43), kind=kOutput, calls=%fused_computation.3 | convolution fusion | flops 1212153856 | bytes 7380996 | tf_op jit(solution)/shard_map/dot_general | solution.py:50
  157.1 0.0 copy-start.4
  157.2 75.4 %fusion = f32[80,272]{1,0:T(8,128)S(1)} fusion(f32[2176,272]{1,0:T(8,128)S(1)} %fusion.1), kind=kCustom, calls=%all-reduce-scatter | all-reduce-scatter fusion | flops 696321 | bytes 2455552
  232.6 4.4 %collective-permute-start.3 = (f32[80,272]{1,0:T(8,128)S(1)}, f32[80,272]{1,0:T(8,128)S(1)}, u32[]{:S(2)}, u32[]{:S(2)}) collective-permute-start(f32[80,272]{1,0:T(8,128)S(1)} %fusion), channel_id=1, source_target_pairs={{0,4},{1,5},{2,6},{3,7},{4,8},{5,9},{6,10},{7,11},{8,12},{9,13},{1... | collective-permute-start | bytes 261128
  236.9 8.4 %collective-permute-start.2 = (f32[80,272]{1,0:T(8,128)S(1)}, f32[80,272]{1,0:T(8,128)S(1)}, u32[]{:S(2)}, u32[]{:S(2)}) collective-permute-start(f32[80,272]{1,0:T(8,128)S(1)} %fusion), channel_id=1, source_target_pairs={{0,3},{1,4},{2,5},{3,6},{4,7},{5,8},{6,9},{7,10},{8,11},{9,12},{10... | collective-permute-start | bytes 261128
  245.3 10.9 %collective-permute-start.1 = (f32[80,272]{1,0:T(8,128)S(1)}, f32[80,272]{1,0:T(8,128)S(1)}, u32[]{:S(2)}, u32[]{:S(2)}) collective-permute-start(f32[80,272]{1,0:T(8,128)S(1)} %fusion), channel_id=1, source_target_pairs={{0,2},{1,3},{2,4},{3,5},{4,6},{5,7},{6,8},{7,9},{8,10},{9,11},{10,... | collective-permute-start | bytes 261128
  256.3 8.4 %collective-permute-start = (f32[80,272]{1,0:T(8,128)S(1)}, f32[80,272]{1,0:T(8,128)S(1)}, u32[]{:S(2)}, u32[]{:S(2)}) collective-permute-start(f32[80,272]{1,0:T(8,128)S(1)} %fusion), channel_id=1, source_target_pairs={{0,1},{1,2},{2,3},{3,4},{4,5},{5,6},{6,7},{7,8},{8,9},{9,10},{10,1... | collective-permute-start | bytes 261128
  264.7 1.9 collective-permute-start.4
  266.6 0.6 dynamic-slice.4
  267.9 4.8 %collective-permute-done.4 = f32[52,272]{1,0:T(8,128)S(1)} collective-permute-done((f32[52,272]{1,0:T(8,128)S(1)}, f32[52,272]{1,0:T(8,128)S(1)}, u32[]{:S(2)}, u32[]{:S(2)}) %collective-permute-start.4) | collective-permute-done | bytes 56608
  272.6 0.0 collective-permute-done.3
  272.7 1.0 concatenate.50
  273.7 0.7 dynamic-slice_multiply_fusion
  (23 shorter events, 0.1 us)
Async XLA Ops:
  6.5 21.7 %copy-start.2 = (s32[1,128]{1,0:T(1,128)S(1)}, s32[1,128]{1,0:T(1,128)}, u32[]{:S(2)}) copy-start(s32[1,128]{1,0:T(1,128)} %param.5) | copy-start | bytes 1540
  28.2 48.4 %copy-start.1 = (f32[32]{0:T(128)S(1)}, f32[32]{0:T(128)}, u32[]{:S(2)}) copy-start(f32[32]{0:T(128)} %param.6) | copy-start | bytes 388
  28.2 48.4 %copy-start.3 = (s32[31]{0:T(128)S(1)}, s32[31]{0:T(128)}, u32[]{:S(2)}) copy-start(s32[31]{0:T(128)} %param.7) | copy-start | bytes 376
  70.1 11.5 %all-to-all-start = ((f32[8,1,2048]{2,1,0:T(1,128)}), f32[8,1,2048]{2,1,0:T(1,128)S(1)}, u32[]{:S(2)}, u32[]{:S(2)}) async-start(f32[8,1,2048]{2,1,0:T(1,128)} %reshape.135), calls=%async_computation | async-start | bytes 131072 | tf_op jit(solution)/shard_map/all_to_all | solution.py:42
  76.6 75.6 %all-gather.2.cloned.1.call-start = ((), (), s32[]{:S(2)}) async-start(), calls=%async_computation.1 | async-start | bytes 5013504 | tf_op jit(solution)/shard_map/all_gather | solution.py:48
  86.8 0.8 copy-start
  157.1 109.5 %copy-start.4 = (u32[256]{0:T(256)S(1)}, u32[256]{0:T(256)}, u32[]{:S(2)}) copy-start(u32[256]{0:T(256)} %constant.76) | copy-start | bytes 3076
  232.6 40.1 %collective-permute-start.3 = (f32[80,272]{1,0:T(8,128)S(1)}, f32[80,272]{1,0:T(8,128)S(1)}, u32[]{:S(2)}, u32[]{:S(2)}) collective-permute-start(f32[80,272]{1,0:T(8,128)S(1)} %fusion), channel_id=1, source_target_pairs={{0,4},{1,5},{2,6},{3,7},{4,8},{5,9},{6,10},{7,11},{8,12},{9,13},{1... | collective-permute-start | bytes 261128
  236.9 35.7 %collective-permute-start.2 = (f32[80,272]{1,0:T(8,128)S(1)}, f32[80,272]{1,0:T(8,128)S(1)}, u32[]{:S(2)}, u32[]{:S(2)}) collective-permute-start(f32[80,272]{1,0:T(8,128)S(1)} %fusion), channel_id=1, source_target_pairs={{0,3},{1,4},{2,5},{3,6},{4,7},{5,8},{6,9},{7,10},{8,11},{9,12},{10... | collective-permute-start | bytes 261128
  245.3 27.3 %collective-permute-start.1 = (f32[80,272]{1,0:T(8,128)S(1)}, f32[80,272]{1,0:T(8,128)S(1)}, u32[]{:S(2)}, u32[]{:S(2)}) collective-permute-start(f32[80,272]{1,0:T(8,128)S(1)} %fusion), channel_id=1, source_target_pairs={{0,2},{1,3},{2,4},{3,5},{4,6},{5,7},{6,8},{7,9},{8,10},{9,11},{10,... | collective-permute-start | bytes 261128
  256.3 16.4 %collective-permute-start = (f32[80,272]{1,0:T(8,128)S(1)}, f32[80,272]{1,0:T(8,128)S(1)}, u32[]{:S(2)}, u32[]{:S(2)}) collective-permute-start(f32[80,272]{1,0:T(8,128)S(1)} %fusion), channel_id=1, source_target_pairs={{0,1},{1,2},{2,3},{3,4},{4,5},{5,6},{6,7},{7,8},{8,9},{9,10},{10,1... | collective-permute-start | bytes 261128
  264.7 7.9 %collective-permute-start.4 = (f32[52,272]{1,0:T(8,128)S(1)}, f32[52,272]{1,0:T(8,128)S(1)}, u32[]{:S(2)}, u32[]{:S(2)}) collective-permute-start(f32[52,272]{1,0:T(8,128)S(1)} %slice.42), channel_id=1, source_target_pairs={{0,5},{1,6},{2,7},{3,8},{4,9},{5,10},{6,11},{7,12},{8,13},{9,14},{... | collective-permute-start | bytes 169736
Sparse Core Ops, SparseCore 0:
  87.8 64.4 all-gather.1
where the time goes:
time: 284 us; the launch traced here: 281 us
  blocking collectives  91.9 us (32%)
  waiting for transfers between devices  74.1 us (26%)
  local copies, waits for them, and re-layouts  48.2 us (17%)
  starting transfers between devices  40.6 us (14%)
  between operations  14.3 us (5%)
  other arithmetic  7.31 us (3%)
  matrix products  4.9 us (2%)
    unnamed x1, blocking collectives  75.4 us
    all_gather x1, waiting for transfers between devices, on_device(): block_features_bf = lax.all_gather(features_bf, 'lev', axis=1, tiled=True)  64.6 us
    unnamed x5, starting transfers between devices  34 us
    unnamed x20, local copies, waits for them, and re-layouts  30 us
    gather x1, local copies, waits for them, and re-layouts, on_device(): chosen = jnp.take(slab_fields, offsets, axis=2)  16.8 us
    all_gather x1, blocking collectives, on_device(): all_lists = lax.all_gather(sample_index, 'lev', axis=1, tiled=True)[0]  16.4 us
    all_to_all x1, starting transfers between devices, on_device(): lax.all_to_all(chosen, 'lev', split_axis=2, concat_axis=1, tiled=True)  6.56 us
  transfers between devices with their start and end apart: 7, of which 3 were waited for; matrix products, arithmetic and copies ran while one was open for 0% of the time, Pallas kernels for 0%

commit v1 on v0

--- a/solution.py
+++ b/solution.py
@@ -45,7 +45,9 @@
     col_count = feat_count // lev_count
     col_start = lax.axis_index("lev") * col_count
     features_bf = quadratic_features(smooth)
-    block_features_bf = lax.all_gather(features_bf, "lev", axis=1, tiled=True)
+    block_features_bf = jnp.concatenate(
+        lax.all_to_all(jnp.stack([features_bf] * lax.axis_size("lev")), "lev", 0, 0), axis=1
+    )
     chosen_rows = lax.dynamic_slice_in_dim(block_features_bf, col_start, col_count, 0)
     column_block = lax.dot_general(
         block_features_bf, chosen_rows, (((1,), (1,)), ((), ())), preferred_element_type=jnp.float32

time: 284 us -> 259 us (0.912)
  the two profiles are of different devices: /device:TPU:26 before, /device:TPU:30 now
where the time goes in v1:
time: 259 us; the launch traced here: 257 us
  blocking collectives  91.8 us (35%)
  waiting for transfers between devices  54 us (21%)
  local copies, waits for them, and re-layouts  50.3 us (19%)
  starting transfers between devices  47.1 us (18%)
  other arithmetic  7.31 us (3%)
  matrix products  5.15 us (2%)
    unnamed x1, blocking collectives  76.9 us
    all_to_all x1, waiting for transfers between devices, on_device(): lax.all_to_all(jnp.stack([features_bf] * lax.axis_size('lev')), 'lev', 0, 0)  45.1 us
    unnamed x5, starting transfers between devices  32.5 us
    unnamed x18, local copies, waits for them, and re-layouts  29.1 us
    gather x1, local copies, waits for them, and re-layouts, on_device(): chosen = jnp.take(slab_fields, offsets, axis=2)  16.8 us
    all_gather x1, blocking collectives, on_device(): all_lists = lax.all_gather(sample_index, 'lev', axis=1, tiled=True)[0]  14.9 us
    all_to_all x1, starting transfers between devices, on_device(): lax.all_to_all(chosen, 'lev', split_axis=2, concat_axis=1, tiled=True)  8.08 us
    all_to_all x1, starting transfers between devices, on_device(): lax.all_to_all(jnp.stack([features_bf] * lax.axis_size('lev')), 'lev', 0, 0)  6.54 us
  transfers between devices with their start and end apart: 7, of which 3 were waited for; matrix products, arithmetic and copies ran while one was open for 0% of the time, Pallas kernels for 0%

profile of v1, /device:TPU:30, one launch (start us, length us, event | category | flops | bytes accessed | tf_op | source)
XLA Modules:
  0.0 256.6 jit_solution(7957375144239462190)
XLA Ops:
  0.0 21.7 %copy.16 = f32[4,4,16384]{1,0,2:T(4,128)} copy(f32[4,4,16384]{2,1,0:T(4,128)} %param.4) | data formatting | bytes 2097152 | tf_op args[0]
  21.7 14.9 %all_gather.3 = s32[1,1024]{1,0:T(1,128)S(1)} all-gather(s32[1,128]{1,0:T(1,128)S(1)} %copy-done.1), channel_id=1, replica_groups=mesh['lev'=8,'hor'=32] {'lev'}, dimensions={1}, use_global_device_ids=true | all-gather | bytes 4608 | tf_op jit(solution)/shard_map/all_gather | solution.py:38
  36.6 16.8 %gather_fusion = f32[1024,4,4]{2,1,0:T(4,128)} fusion(f32[4,4,16384]{1,0,2:T(4,128)} %copy.16, s32[1024]{0:T(1024)S(1)} %broadcast_clamp_fusion), kind=kCustom, calls=%fused_computation | custom fusion | bytes 135168 | tf_op jit(solution)/shard_map/jit(_take)/gather | solution.py:41
  53.4 5.5 %fusion.18 = f32[1024,4,4]{2,1,0:T(4,128)S(1)} fusion(f32[1024,4,4]{2,1,0:T(4,128)} %gather_fusion, pred[1024]{0:T(1024)(128)(4,1)S(1)} %compare_and_fusion), kind=kLoop, calls=%fused_computation.49 | loop fusion | flops 16384 | bytes 132096
  58.9 3.0 %reshape.164 = f32[8,1,2048]{2,1,0:T(1,128)} reshape(f32[1024,4,4]{2,1,0:T(4,128)S(1)} %fusion.18) | data formatting | bytes 131072
  61.9 8.1 %all-to-all-start = ((f32[8,1,2048]{2,1,0:T(1,128)}), f32[8,1,2048]{2,1,0:T(1,128)S(1)}, u32[]{:S(2)}, u32[]{:S(2)}) async-start(f32[8,1,2048]{2,1,0:T(1,128)} %reshape.164), calls=%async_computation | async-start | bytes 131072 | tf_op jit(solution)/shard_map/all_to_all | solution.py:42
  70.0 0.1 fusion.17
  70.1 0.1 add_add_fusion
  70.2 4.1 %all-to-all-done = f32[8,1,2048]{2,1,0:T(1,128)S(1)} async-done(((f32[8,1,2048]{2,1,0:T(1,128)}), f32[8,1,2048]{2,1,0:T(1,128)S(1)}, u32[]{:S(2)}, u32[]{:S(2)}) %all-to-all-start) | async-done | bytes 65568 | tf_op jit(solution)/shard_map/all_to_all | solution.py:42
  74.3 0.5 broadcast.123
  74.8 0.8 reduce
  75.6 2.7 %reshape.165 = f32[1024,4,4]{2,1,0:T(4,128)S(1)} reshape(f32[8,2048]{1,0:T(8,128)S(1)} %reduce) | data formatting | bytes 131072
  78.4 0.8 copy.17
  79.2 0.1 add_divide_fusion
  79.4 0.1 multiply_convert_fusion
  79.5 0.1 constant_dynamic-update-slice_fusion
  79.6 0.3 copy.18
  79.9 2.7 %stack.2 = bf16[8,2176,128]{1,2,0:T(8,128)(2,1)} broadcast(bf16[2176,128]{0,1:T(8,128)(2,1)S(1)} %copy.18), dimensions={1,2} | broadcast | bytes 5013504 | tf_op jit(solution)/shard_map/stack | solution.py:49
  82.5 6.5 %all-to-all-start.1 = ((bf16[8,2176,128]{1,2,0:T(8,128)(2,1)}), bf16[8,2176,128]{1,2,0:T(8,128)(2,1)}, u32[]{:S(2)}, u32[]{:S(2)}) async-start(bf16[8,2176,128]{1,2,0:T(8,128)(2,1)} %stack.2), calls=%async_computation.1 | async-start | bytes 8912896 | tf_op jit(solution)/shard_map/all_to_all | solution.py:49
  89.1 45.1 %all-to-all-done.1 = bf16[8,2176,128]{1,2,0:T(8,128)(2,1)} async-done(((bf16[8,2176,128]{1,2,0:T(8,128)(2,1)}), bf16[8,2176,128]{1,2,0:T(8,128)(2,1)}, u32[]{:S(2)}, u32[]{:S(2)}) %all-to-all-start.1) | async-done | bytes 4456480 | tf_op jit(solution)/shard_map/all_to_all | solution.py:49
  134.2 5.1 %fusion.1 = f32[2176,272]{1,0:T(8,128)S(1)} fusion(bf16[2176,1024]{0,1:T(8,128)(2,1)} %bitcast.14, s32[]{:T(128)S(6)} %select_n.43), kind=kOutput, calls=%fused_computation.3 | convolution fusion | flops 1212153856 | bytes 7610372 | tf_op jit(solution)/shard_map/dot_general | solution.py:52
  139.3 0.0 copy-start.3
  139.4 76.9 %fusion = f32[80,272]{1,0:T(8,128)S(1)} fusion(f32[2176,272]{1,0:T(8,128)S(1)} %fusion.1), kind=kCustom, calls=%all-reduce-scatter | all-reduce-scatter fusion | flops 696321 | bytes 2455552
  216.3 7.7 %collective-permute-start.3 = (f32[80,272]{1,0:T(8,128)S(1)}, f32[80,272]{1,0:T(8,128)S(1)}, u32[]{:S(2)}, u32[]{:S(2)}) collective-permute-start(f32[80,272]{1,0:T(8,128)S(1)} %fusion), channel_id=1, source_target_pairs={{0,4},{1,5},{2,6},{3,7},{4,8},{5,9},{6,10},{7,11},{8,12},{9,13},{1... | collective-permute-start | bytes 261128
  224.0 3.9 %collective-permute-start.2 = (f32[80,272]{1,0:T(8,128)S(1)}, f32[80,272]{1,0:T(8,128)S(1)}, u32[]{:S(2)}, u32[]{:S(2)}) collective-permute-start(f32[80,272]{1,0:T(8,128)S(1)} %fusion), channel_id=1, source_target_pairs={{0,3},{1,4},{2,5},{3,6},{4,7},{5,8},{6,9},{7,10},{8,11},{9,12},{10... | collective-permute-start | bytes 261128
  227.9 10.7 %collective-permute-start.1 = (f32[80,272]{1,0:T(8,128)S(1)}, f32[80,272]{1,0:T(8,128)S(1)}, u32[]{:S(2)}, u32[]{:S(2)}) collective-permute-start(f32[80,272]{1,0:T(8,128)S(1)} %fusion), channel_id=1, source_target_pairs={{0,2},{1,3},{2,4},{3,5},{4,6},{5,7},{6,8},{7,9},{8,10},{9,11},{10,... | collective-permute-start | bytes 261128
  238.6 8.3 %collective-permute-start = (f32[80,272]{1,0:T(8,128)S(1)}, f32[80,272]{1,0:T(8,128)S(1)}, u32[]{:S(2)}, u32[]{:S(2)}) collective-permute-start(f32[80,272]{1,0:T(8,128)S(1)} %fusion), channel_id=1, source_target_pairs={{0,1},{1,2},{2,3},{3,4},{4,5},{5,6},{6,7},{7,8},{8,9},{9,10},{10,1... | collective-permute-start | bytes 261128
  246.9 1.9 collective-permute-start.4
  248.9 0.6 dynamic-slice.4
  250.1 4.8 %collective-permute-done.4 = f32[52,272]{1,0:T(8,128)S(1)} collective-permute-done((f32[52,272]{1,0:T(8,128)S(1)}, f32[52,272]{1,0:T(8,128)S(1)}, u32[]{:S(2)}, u32[]{:S(2)}) %collective-permute-start.4) | collective-permute-done | bytes 56608
  254.9 1.0 concatenate.64
  255.9 0.7 dynamic-slice_multiply_fusion
  (22 shorter events, 0.1 us)
Async XLA Ops:
  0.0 21.7 %copy-start.1 = (s32[1,128]{1,0:T(1,128)S(1)}, s32[1,128]{1,0:T(1,128)}, u32[]{:S(2)}) copy-start(s32[1,128]{1,0:T(1,128)} %param.5) | copy-start | bytes 1540
  21.7 48.3 %copy-start = (f32[32]{0:T(128)S(1)}, f32[32]{0:T(128)}, u32[]{:S(2)}) copy-start(f32[32]{0:T(128)} %param.6) | copy-start | bytes 388
  21.7 48.3 %copy-start.2 = (s32[31]{0:T(128)S(1)}, s32[31]{0:T(128)}, u32[]{:S(2)}) copy-start(s32[31]{0:T(128)} %param.7) | copy-start | bytes 376
  61.9 12.4 %all-to-all-start = ((f32[8,1,2048]{2,1,0:T(1,128)}), f32[8,1,2048]{2,1,0:T(1,128)S(1)}, u32[]{:S(2)}, u32[]{:S(2)}) async-start(f32[8,1,2048]{2,1,0:T(1,128)} %reshape.164), calls=%async_computation | async-start | bytes 131072 | tf_op jit(solution)/shard_map/all_to_all | solution.py:42
  82.5 51.7 %all-to-all-start.1 = ((bf16[8,2176,128]{1,2,0:T(8,128)(2,1)}), bf16[8,2176,128]{1,2,0:T(8,128)(2,1)}, u32[]{:S(2)}, u32[]{:S(2)}) async-start(bf16[8,2176,128]{1,2,0:T(8,128)(2,1)} %stack.2), calls=%async_computation.1 | async-start | bytes 8912896 | tf_op jit(solution)/shard_map/all_to_all | solution.py:49
  139.3 109.5 %copy-start.3 = (u32[256]{0:T(256)S(1)}, u32[256]{0:T(256)}, u32[]{:S(2)}) copy-start(u32[256]{0:T(256)} %constant.76) | copy-start | bytes 3076
  216.3 38.6 %collective-permute-start.3 = (f32[80,272]{1,0:T(8,128)S(1)}, f32[80,272]{1,0:T(8,128)S(1)}, u32[]{:S(2)}, u32[]{:S(2)}) collective-permute-start(f32[80,272]{1,0:T(8,128)S(1)} %fusion), channel_id=1, source_target_pairs={{0,4},{1,5},{2,6},{3,7},{4,8},{5,9},{6,10},{7,11},{8,12},{9,13},{1... | collective-permute-start | bytes 261128
  224.0 30.9 %collective-permute-start.2 = (f32[80,272]{1,0:T(8,128)S(1)}, f32[80,272]{1,0:T(8,128)S(1)}, u32[]{:S(2)}, u32[]{:S(2)}) collective-permute-start(f32[80,272]{1,0:T(8,128)S(1)} %fusion), channel_id=1, source_target_pairs={{0,3},{1,4},{2,5},{3,6},{4,7},{5,8},{6,9},{7,10},{8,11},{9,12},{10... | collective-permute-start | bytes 261128
  227.9 27.0 %collective-permute-start.1 = (f32[80,272]{1,0:T(8,128)S(1)}, f32[80,272]{1,0:T(8,128)S(1)}, u32[]{:S(2)}, u32[]{:S(2)}) collective-permute-start(f32[80,272]{1,0:T(8,128)S(1)} %fusion), channel_id=1, source_target_pairs={{0,2},{1,3},{2,4},{3,5},{4,6},{5,7},{6,8},{7,9},{8,10},{9,11},{10,... | collective-permute-start | bytes 261128
  238.6 16.3 %collective-permute-start = (f32[80,272]{1,0:T(8,128)S(1)}, f32[80,272]{1,0:T(8,128)S(1)}, u32[]{:S(2)}, u32[]{:S(2)}) collective-permute-start(f32[80,272]{1,0:T(8,128)S(1)} %fusion), channel_id=1, source_target_pairs={{0,1},{1,2},{2,3},{3,4},{4,5},{5,6},{6,7},{7,8},{8,9},{9,10},{10,1... | collective-permute-start | bytes 261128
  246.9 7.9 %collective-permute-start.4 = (f32[52,272]{1,0:T(8,128)S(1)}, f32[52,272]{1,0:T(8,128)S(1)}, u32[]{:S(2)}, u32[]{:S(2)}) collective-permute-start(f32[52,272]{1,0:T(8,128)S(1)} %slice.42), channel_id=1, source_target_pairs={{0,5},{1,6},{2,7},{3,8},{4,9},{5,10},{6,11},{7,12},{8,13},{9,14},{... | collective-permute-start | bytes 169736
